TPU v7x, 256 devices: a whole 4x4x8 slice. The times are simulated.
256 devices in a mesh: task: 8 (over x_hi, y), mp: 32 (over x_lo, z, core).
Axes of the slice: x: 4 (x_hi: 2, x_lo: 2; x = x_hi * 2 + x_lo), y: 4, z: 8, core: 2. Of those that a mesh axis runs over, the one named last changes fastest.
Arguments:
- hidden: bfloat16 [8, 2048, 8192], P('task', 'mp'), may hold values from -6 to 6
- gain: float32 [8192], replicated, may hold values from 0.25 to 1.75
- tau: bfloat16 [8, 8192, 1024], P('task', 'mp'), may hold values from -0.0625 to 0.0625
- coeff: float32 [8, 8192, 1024], P('task', 'mp'), may hold values from 0.1 to 1
- counts: int32 [8], P('task'), may hold values from 683 to 2048, as said below
- positions: int32 [8, 2048], P('task', 'mp'), may hold values from 0 to 2047
Outputs:
- grad_coeff: float32 [8, 8192, 1024], P('task', 'mp')
- loss: float32 [], replicated
Inputs may be any that keep to these rules, and one draw needn't show every extreme that they name: `counts`: counts lie between a third of 2048 and 2048; some task has exactly 2048 in every draw. Rows at or past a task's count are not live.
All inputs are finite; a program needn't handle non-finite values.
Results may differ from a plain program's by a relative error of at most 0.0044.
The roundings to bfloat16 on the way count: a program that leaves them out, or rounds other values in their place, can miss the bound.
Values may be sent and summed in bfloat16 or wider, within the bound.
A program may use at most 64 MiB of HBM per device.

v0:
```python
import jax
import jax.numpy as jnp
from jax import lax
from jax.sharding import Mesh
from jax.sharding import PartitionSpec as P

HEAD = 128
MP = ("mp_0", "mp_1", "mp_2")
TASK = ("task_0", "task_1")
TASK_MP = ("task_0", "task_1", "mp_0", "mp_1", "mp_2")


def cut_along(value, dim, length):
    before, after = (value.shape[:dim], value.shape[dim + 1 :])
    return jnp.moveaxis(value.reshape(*before, length, -1, *after), dim, 0)


def scatter_pairs(value, chips, core, dim):
    sizes = (lax.axis_size(chips), lax.axis_size(core))
    tiles = cut_along(value, dim, sizes[0] * sizes[1])
    inside = tiles.shape[1:]
    tiles = tiles.reshape(*sizes, *inside).swapaxes(0, 1).reshape(-1, *inside)
    tiles = lax.psum_scatter(tiles, core, scatter_dimension=0, tiled=True)
    return lax.psum_scatter(tiles, chips, scatter_dimension=0, tiled=True)[0]


def by_axis(value, axes):
    for axis in axes:
        value = lax.psum(value, axis)
    return value


def rotary_tables(positions, head):
    index = jnp.arange(head // 2).astype(jnp.float32)
    freq = jnp.exp(-jnp.log(jnp.float32(1000000.0)) * 2.0 * index / head)
    angle = positions.astype(jnp.float32)[:, None] * freq[None, :]
    return (jnp.cos(angle), jnp.sin(angle))


def rotate(values, cosine, sine, sign, head):
    count = values.shape[0]
    width = values.shape[1]
    shaped = values.reshape(count, width // head, 2, head // 2)
    first = shaped[:, :, 0, :]
    second = shaped[:, :, 1, :]
    cosine = cosine[:, None, :]
    sine = sine[:, None, :] * sign
    out_first = first * cosine - second * sine
    out_second = second * cosine + first * sine
    return jnp.stack([out_first, out_second], axis=2).reshape(count, width)


def local(hidden, gain, tau, coeff, counts, positions):
    rows = hidden[0].astype(jnp.float32)
    width = rows.shape[1]
    keys = tau.shape[2]
    rows_local = rows.shape[0]
    inverse = 1.0 / jnp.sqrt(jnp.mean(rows * rows, axis=1, keepdims=True) + 1e-06)
    normed = (rows * inverse * gain[None, :]).astype(jnp.bfloat16)
    columns = lax.all_to_all(normed, MP, split_axis=1, concat_axis=0, tiled=True)
    tau_local = tau[0].astype(jnp.float32)
    mixed = lax.psum(coeff[0] * tau_local, TASK)
    merged = mixed.astype(jnp.bfloat16)
    teacher = tau[0]
    block = columns
    gap = scatter_pairs(
        jnp.dot(block, merged, preferred_element_type=jnp.float32)
        - jnp.dot(block, teacher, preferred_element_type=jnp.float32),
        ("mp_0", "mp_1"),
        "mp_2",
        0,
    )
    first_row = lax.axis_index(MP) * rows_local
    cosine, sine = rotary_tables(positions[0], HEAD)
    err = rotate(gap, cosine, sine, 1.0, HEAD)
    row_ids = first_row + jnp.arange(rows_local)
    live = (row_ids < counts[0]).astype(jnp.float32)[:, None]
    scale = 1.0 / (counts[0].astype(jnp.float32) * keys)
    partial_loss = jnp.sum(live * err * err) * scale
    back = rotate(2.0 * scale * live * err, cosine, sine, -1.0, HEAD).astype(jnp.bfloat16)
    block = columns
    local_grad = lax.dot_general(
        block,
        lax.all_gather(back, MP, axis=0, tiled=True),
        (((0,), (0,)), ((), ())),
        preferred_element_type=jnp.float32,
    )
    wgrad = lax.psum(local_grad, TASK)
    loss = by_axis(partial_loss, TASK_MP)
    grad_coeff = width * keys * tau_local * wgrad
    return (grad_coeff[None, :, :], loss)


def solution(mesh):
    split = Mesh(mesh.devices.reshape(2, 4, 2, 8, 2), ("task_0", "task_1", "mp_0", "mp_1", "mp_2"))
    placed = (P(TASK, MP, None), P(), P(TASK, MP, None), P(TASK, MP, None), P(TASK), P(TASK, MP))
    return jax.shard_map(
        local, mesh=split, in_specs=placed, out_specs=(P(TASK, MP, None), P()), check_vma=False
    )
```

profile of v0, /device:TPU:1, one launch (start us, length us, event | category | flops | bytes accessed | tf_op | source)
XLA Modules:
  0.0 387.4 jit_solution(13827501548182623606)
XLA Ops:
  7.2 1.5 multiply_reduce_fusion
  8.7 1.5 copy.13
  10.6 1.6 copy.11
  12.1 11.0 %all-to-all-start = ((bf16[64,32,256]{2,0,1:T(8,128)(2,1)}), bf16[64,32,256]{2,0,1:T(8,128)(2,1)S(1)}, u32[]{:S(2)}, u32[]{:S(2)}) async-start(bf16[64,32,256]{2,0,1:T(8,128)(2,1)} %copy.11), calls=%async_computation | async-start | bytes 2097152 | tf_op jit(solution)/shard_map/all_to_all | solution.py:60
  23.2 1.4 convert_multiply_fusion
  24.6 71.5 %all-reduce.4 = bf16[256,1024]{1,0:T(8,128)(2,1)S(1)} all-reduce(f32[256,1024]{1,0:T(8,128)S(1)} %convert_multiply_fusion), channel_id=1, replica_groups=mesh['task_0'=2,'task_1'=4,'mp_0'=2,'mp_1'=8,'mp_2'=2] {'task_0','task_1'}, use_global_device_ids=true, to_apply=%region_1.0 | all-reduce | flops 262144 | bytes 1572864 | tf_op jit(solution)/shard_map/psum | solution.py:62
  96.1 1.3 fusion.9
  97.4 1.3 convolution_subtract_fusion
  98.7 4.1 %copy.12 = f32[16,2,64,1024]{3,2,0,1:T(8,128)} copy(f32[16,2,64,1024]{3,2,1,0:T(8,128)S(1)} %bitcast.36) | data formatting | bytes 16777216 | tf_op jit(solution)/shard_map/reshape;reshape | solution.py:22
  102.8 30.5 %reduce-scatter.3.cloned.1.call-done = f32[16,64,1024]{2,1,0:T(8,128)} async-done(((f32[32,64,1024]{2,1,0:T(8,128)}), f32[16,64,1024]{2,1,0:T(8,128)}) %reduce-scatter.3.cloned.1.call-update) | async-done | bytes 4194320 | tf_op jit(solution)/shard_map/reduce_scatter | solution.py:23
  134.3 72.8 %reduce-scatter.5.cloned.1.call-done = f32[1,64,1024]{2,1,0:T(8,128)} async-done(((f32[16,64,1024]{2,1,0:T(8,128)}), f32[1,64,1024]{2,1,0:T(8,128)}) %reduce-scatter.5.cloned.1.call-update) | async-done | bytes 262160 | tf_op jit(solution)/shard_map/reduce_scatter | solution.py:24
  207.2 1.3 reshape_squeeze.3
  209.1 1.8 fusion.4
  211.6 0.7 pad_maximum_fusion.1
  212.3 0.9 convert_element_type.62
  213.2 73.8 %all-gather.2.cloned.1.call-done = bf16[2048,1024]{1,0:T(8,128)(2,1)} async-done(((bf16[64,1024]{1,0:T(8,128)(2,1)}), bf16[2048,1024]{1,0:T(8,128)(2,1)}) %all-gather.2.cloned.1.call-update) | async-done | bytes 4194320 | tf_op jit(solution)/shard_map/all_gather | solution.py:84
  287.0 4.4 %fusion.8 = f32[256,1024]{1,0:T(8,128)} fusion(bf16[2048,256]{1,0:T(8,128)(2,1)S(1)} %bitcast.40, bf16[2048,1024]{1,0:T(8,128)(2,1)} %all-gather.2.cloned.1.call-done), kind=kOutput, calls=%fused_computation.30 | convolution fusion | flops 1073741824 | bytes 6291456 | tf_op jit(solution)/shard_map/dot_general | solution.py:82
  292.2 5.8 %psum.51 = f32[]{:T(128)} all-reduce(f32[]{:T(128)S(6)} %mul.221), channel_id=1, replica_groups=mesh['task_0'=2,'task_1'=4,'mp_0'=2,'mp_1'=8,'mp_2'=2] {'task_0'}, use_global_device_ids=true, to_apply=%region_6.0 | all-reduce | flops 1 | bytes 8 | tf_op jit(solution)/shard_map/psum | solution.py:29
  297.9 9.1 %psum.52 = f32[]{:T(128)} all-reduce(f32[]{:T(128)} %psum.51), channel_id=1, replica_groups=mesh['task_0'=2,'task_1'=4,'mp_0'=2,'mp_1'=8,'mp_2'=2] {'task_1'}, use_global_device_ids=true, to_apply=%region_7.0 | all-reduce | flops 1 | bytes 8 | tf_op jit(solution)/shard_map/psum | solution.py:29
  307.0 4.8 %psum.53 = f32[]{:T(128)} all-reduce(f32[]{:T(128)} %psum.52), channel_id=1, replica_groups=mesh['task_0'=2,'task_1'=4,'mp_0'=2,'mp_1'=8,'mp_2'=2] {'mp_0'}, use_global_device_ids=true, to_apply=%region_8.0 | all-reduce | flops 1 | bytes 8 | tf_op jit(solution)/shard_map/psum | solution.py:29
  311.8 13.6 %psum.54 = f32[]{:T(128)} all-reduce(f32[]{:T(128)} %psum.53), channel_id=1, replica_groups=mesh['task_0'=2,'task_1'=4,'mp_0'=2,'mp_1'=8,'mp_2'=2] {'mp_1'}, use_global_device_ids=true, to_apply=%region_9.0 | all-reduce | flops 1 | bytes 8 | tf_op jit(solution)/shard_map/psum | solution.py:29
  325.4 9.9 %psum.55 = f32[]{:T(128)} all-reduce(f32[]{:T(128)} %psum.54), channel_id=1, replica_groups=mesh['task_0'=2,'task_1'=4,'mp_0'=2,'mp_1'=8,'mp_2'=2] {'mp_2'}, use_global_device_ids=true, to_apply=%region_10.0 | all-reduce | flops 1 | bytes 8 | tf_op jit(solution)/shard_map/psum | solution.py:29
  335.3 43.2 %all-reduce.3.cloned.1.call-done = f32[256,1024]{1,0:T(8,128)} async-done(((f32[256,1024]{1,0:T(8,128)}), f32[256,1024]{1,0:T(8,128)}) %all-reduce.3.cloned.1.call-update) | async-done | bytes 1048592 | tf_op jit(solution)/shard_map/psum | solution.py:88
  378.5 2.4 fusion.3
  (25 shorter events, 2.0 us)
Async XLA Ops:
  7.2 3.1 copy-start.1
  10.2 13.0 %copy-start = (bf16[1,256,1024]{2,1,0:T(8,128)(2,1)S(1)}, bf16[1,256,1024]{2,1,0:T(8,128)(2,1)}, u32[]{:S(2)}) copy-start(bf16[1,256,1024]{2,1,0:T(8,128)(2,1)} %param.8) | copy-start | bytes 1572868
  12.1 84.0 %all-to-all-start = ((bf16[64,32,256]{2,0,1:T(8,128)(2,1)}), bf16[64,32,256]{2,0,1:T(8,128)(2,1)S(1)}, u32[]{:S(2)}, u32[]{:S(2)}) async-start(bf16[64,32,256]{2,0,1:T(8,128)(2,1)} %copy.11), calls=%async_computation | async-start | bytes 2097152 | tf_op jit(solution)/shard_map/all_to_all | solution.py:60
  23.2 110.1 %reduce-scatter.3.cloned.1.call-start = ((), (), s32[]{:S(2)}) async-start(), calls=%async_computation.3 | async-start | bytes 12582912 | tf_op jit(solution)/shard_map/reduce_scatter | solution.py:23
  102.7 31.4 %copy-start.2 = (s32[1,64]{1,0:T(1,128)S(1)}, s32[1,64]{1,0:T(1,128)}, u32[]{:S(2)}) copy-start(s32[1,64]{1,0:T(1,128)} %param.11) | copy-start | bytes 772
  102.8 104.4 %reduce-scatter.5.cloned.1.call-start = ((), (), s32[]{:S(2)}) async-start(), calls=%async_computation.4 | async-start | bytes 4456448 | tf_op jit(solution)/shard_map/reduce_scatter | solution.py:24
  133.3 153.7 %all-gather.2.cloned.1.call-start = ((), (), s32[]{:S(2)}) async-start(), calls=%async_computation.5 | async-start | bytes 4325376 | tf_op jit(solution)/shard_map/all_gather | solution.py:84
  213.1 165.4 %all-reduce.3.cloned.1.call-start = ((), (), s32[]{:S(2)}) async-start(), calls=%async_computation.6 | async-start | bytes 2097152 | tf_op jit(solution)/shard_map/psum | solution.py:88
Sparse Core Ops, SparseCore 0:
  102.9 30.3 reduce-scatter.2
  135.8 71.2 reduce-scatter.4
  213.3 73.7 all-gather.1
  291.6 86.8 all-reduce.2
where the time goes:
time: 392 us; the launch traced here: 387 us
  waiting for transfers between devices  220 us (56%)
  blocking collectives  115 us (29%)
  between operations  15.3 us (4%)
  starting transfers between devices  11.2 us (3%)
  other arithmetic  9.5 us (2%)
  local copies, waits for them, and re-layouts  9.36 us (2%)
  matrix products  6.94 us (2%)
    all_gather x1, waiting for transfers between devices, local(): lax.all_gather(back, MP, axis=0, tiled=True)  73.8 us
    reduce_scatter x1, waiting for transfers between devices, scatter_pairs(): return lax.psum_scatter(tiles, chips, scatter_dimension=0, tiled=True)[0]  72.8 us
    psum x1, blocking collectives, local(): mixed = lax.psum(coeff[0] * tau_local, TASK)  71.5 us
    psum x1, waiting for transfers between devices, local(): wgrad = lax.psum(local_grad, TASK)  43.2 us
    psum x5, blocking collectives, by_axis(): value = lax.psum(value, axis)  43.1 us
    reduce_scatter x1, waiting for transfers between devices, scatter_pairs(): tiles = lax.psum_scatter(tiles, core, scatter_dimension=0, tiled=True)  30.5 us
    all_to_all x1, starting transfers between devices, local(): lax.all_to_all(normed, MP, split_axis=1, concat_axis=0, tiled=True)  11 us
  transfers between devices with their start and end apart: 5, of which 4 were waited for; matrix products, arithmetic and copies ran while one was open for 0% of the time, Pallas kernels for 0%

commit v1 on v0

v1 whole, which is shorter than its diff:
```python
import functools

import jax
import jax.numpy as jnp
from jax import lax
from jax.experimental import pallas as pl
from jax.experimental.pallas import tpu as pltpu
from jax.sharding import PartitionSpec as P

MESH = pl.DeviceIdType.MESH
BF = jnp.bfloat16
F32 = jnp.float32
HEAD = 128
SIZES = dict(xh=2, y=4, xl=2, z=8, c=2)
GROUP = (dict(c=1), dict(xl=1), dict(xl=1, c=1))
TASKS = tuple((a, b) for a in (1, 0) for b in (2, 1, 3, 0) if (a, b) != (0, 0))
RING = (4, 3, 5, 2, 6, 1, 7)
N_SEM = 128


class Links:
    def __init__(self, here, send, recv):
        self.here, self.send, self.recv, self.used, self.open = here, send, recv, 0, []

    def peer(self, **offsets):
        p = dict(self.here)
        for axis, by in offsets.items():
            p[axis] = lax.rem(p[axis] + (by % SIZES[axis]), SIZES[axis])
        return p

    def device(self, p):
        return (p["xh"] * 4 + p["y"], p["xl"] * 16 + p["z"] * 2 + p["c"])

    def copy(self, src, dst, p):
        i = self.used
        self.used += 1
        made = pltpu.make_async_remote_copy(
            src_ref=src,
            dst_ref=dst,
            send_sem=self.send.at[i],
            recv_sem=self.recv.at[i],
            device_id=self.device(p),
            device_id_type=MESH,
        )
        made.start()
        self.open.append(made)
        return made

    def drain(self):
        for made in self.open:
            made.wait_send()


def nt(a, b):
    return lax.dot_general(a, b, (((1,), (1,)), ((), ())), preferred_element_type=F32)


def kernel(
    counts,
    hidden,
    gain,
    tau,
    coeff,
    pos,
    w_out,
    loss_out,
    ns,
    a_all,
    tau_own,
    tau_t,
    m_own,
    m_recv,
    m_half,
    m_recv2,
    m_piece,
    merged,
    gap,
    rs_send,
    rs_recv,
    back,
    w_acc,
    w_send,
    w_recv,
    w_piece,
    w_all,
    pos_all,
    loss_z,
    loss_g,
    loss_t,
    send_sem,
    recv_sem,
    local_sem,
):
    t, m = lax.axis_index("task"), lax.axis_index("mp")
    me = dict(
        xh=lax.div(t, 4),
        y=lax.rem(t, 4),
        xl=lax.div(m, 16),
        z=lax.rem(lax.div(m, 2), 8),
        c=lax.rem(m, 2),
    )
    net = Links(me, send_sem, recv_sem)
    xl, z, c, y, xh = me["xl"], me["z"], me["c"], me["y"], me["xh"]
    g = xl * 2 + c

    barrier = pltpu.get_barrier_semaphore()
    partners = [dict(z=d) for d in RING] + list(GROUP) + [dict(xh=a, y=b) for a, b in TASKS]
    for offsets in partners:
        pl.semaphore_signal(
            barrier, inc=1, device_id=net.device(net.peer(**offsets)), device_id_type=MESH
        )

    total = jnp.zeros((64, 1), F32)
    for k in range(8):
        x = hidden[:, k * 1024 : (k + 1) * 1024].astype(F32)
        total = total + jnp.sum(x * x, axis=1, keepdims=True)
    inverse = 1.0 / jnp.sqrt(total * (1.0 / 8192.0) + 1e-06)
    for k in range(8):
        for half in range(2):
            at = half * 4096 + k * 512
            x = hidden[:, at : at + 512].astype(F32)
            ns[k, :, half * 512 : (half + 1) * 512] = (
                x * inverse * gain[:, at : at + 512]
            ).astype(BF)

    pl.semaphore_wait(barrier, len(partners))

    from_z = []
    for d in RING:
        p = net.peer(z=d)
        from_z.append(net.copy(ns.at[p["z"]], a_all.at[z, xl, c], p))
    sib, xn = net.peer(c=1), net.peer(xl=1)
    own_slot = a_all.at[z, xl, c]
    keep = pltpu.make_async_copy(ns.at[z], own_slot, local_sem.at[0])
    keep.start()
    to_sib, to_x = [], []
    to_sib.append(net.copy(ns.at[z], own_slot, sib))
    to_x.append(net.copy(ns.at[z], own_slot, xn))

    lanes = lax.broadcasted_iota(jnp.int32, (8, 128), 1)
    pos_all[xl, c] = jnp.where(
        lax.div(lanes, 64) == c, jnp.broadcast_to(pos[...], (8, 128)), 0
    )
    small = []
    for offsets in GROUP:
        small.append(net.copy(pos_all.at[xl, c], pos_all.at[xl, c], net.peer(**offsets)))

    for k in range(8):
        cut = slice(k * 128, (k + 1) * 128)
        tau_f = tau[:, cut].astype(F32)
        mixed_t = (coeff[:, cut] * tau_f).T
        m_own[k // 2, 2 * (k % 2) : 2 * (k % 2) + 2] = mixed_t.reshape(2, 2, 32, 256)
        tau_own[k // 2, (k % 2) * 128 : (k % 2) * 128 + 128] = tau_f.T.astype(BF)

    from_y = []
    for i, d in enumerate((2, 1, 3)):
        p = net.peer(y=d)
        from_y.append(net.copy(m_own.at[:, p["y"]], m_recv.at[i], p))
    features = pl.ds(pl.multiple_of(g * 256, 256), 256)
    from_tau = []
    for offsets in GROUP:
        p = net.peer(**offsets)
        from_tau.append(net.copy(tau_own.at[p["xl"] * 2 + p["c"]], tau_t.at[:, features], p))
    keep_tau = pltpu.make_async_copy(tau_own.at[g], tau_t.at[:, features], local_sem.at[1])
    keep_tau.start()

    def forward(i):
        from_z[i].wait_recv()
        slot = a_all.at[lax.rem(z + (8 - RING[i]), 8), xl, c]
        to_sib.append(net.copy(slot, slot, sib))
        to_x.append(net.copy(slot, slot, xn))

    def pass_on(i):
        to_x[i].wait_recv()
        origin = z if i == 0 else lax.rem(z + (8 - RING[i - 1]), 8)
        slot = a_all.at[origin, 1 - xl, c]
        second.append(net.copy(slot, slot, sib))

    second = []
    pass_on(0)
    forward(0)
    forward(1)
    pass_on(1)

    for copy in small:
        copy.wait_recv()
    pos_rows = jnp.concatenate([pos_all[0, 0] + pos_all[0, 1], pos_all[1, 0] + pos_all[1, 1]], axis=1)
    index = lax.broadcasted_iota(jnp.int32, (64, 256), 0).astype(F32)
    freq = jnp.exp(-jnp.log(F32(1000000.0)) * 2.0 * index / HEAD)
    angle = pos_rows[0:1].astype(F32) * freq
    cosine, sine = jnp.cos(angle), jnp.sin(angle)

    forward(2)
    pass_on(2)
    forward(3)
    pass_on(3)

    for copy in from_y:
        copy.wait_recv()
    m_half[...] = m_own[:, pl.ds(y, 1)].reshape(4, 2, 32, 256) + m_recv[0] + m_recv[1] + m_recv[2]
    xo = net.peer(xh=1)
    from_xh = net.copy(m_half.at[:, xo["xh"]], m_recv2, xo)

    forward(4)
    pass_on(4)

    from_xh.wait_recv()
    m_piece[...] = (m_half[:, pl.ds(xh, 1)].reshape(4, 32, 256) + m_recv2[...]).astype(BF)
    piece = merged.at[y, xh]
    keep_m = pltpu.make_async_copy(m_piece.at[g], piece.at[:, features], local_sem.at[2])
    keep_m.start()
    from_group = []
    for offsets in GROUP:
        p = net.peer(**offsets)
        from_group.append(net.copy(m_piece.at[p["xl"] * 2 + p["c"]], piece.at[:, features], p))

    forward(5)
    pass_on(5)

    keep_m.wait()
    for copy in from_group:
        copy.wait_recv()
    from_xh2 = net.copy(piece, piece, xo)

    forward(6)
    pass_on(6)

    from_xh2.wait_recv()
    from_y2 = []
    for d in (2, 1, 3):
        from_y2.append(net.copy(merged.at[y], merged.at[y], net.peer(y=d)))
    pass_on(7)

    keep.wait()
    keep_tau.wait()
    for copy in from_tau + to_sib + second + from_y2:
        copy.wait_recv()

    def partial_gap(d):
        zd = lax.rem(z + d, 8)
        rows = a_all[pl.ds(zd, 1)].reshape(256, 1024)
        gap[zd] = nt(merged[...].reshape(256, 1024), rows) - nt(tau_t[...], rows)

    sides = ((0, 1), (1, 7))
    from_rs = {}

    def rs_step(step):
        d = 5 - step
        for h in range(2):
            for s, by in sides:
                zd = lax.rem(z + (by * d) % 8, 8)
                half = slice(s * 64, s * 64 + 64)
                out = rs_send.at[h, s, step - 1]
                if step == 1:
                    at = h * 128 + s * 64
                    out[half] = gap[zd, at : at + 64].astype(BF)
                elif step == 2:
                    from_rs[h, s, 1].wait_recv()
                    other = 1 - s
                    at = h * 128 + s * 64
                    out[half] = (
                        gap[zd, at : at + 64] + rs_recv[h, s, 0, half].astype(F32)
                    ).astype(BF)
                    at = h * 128 + other * 64
                    out[other * 64 : other * 64 + 64] = gap[zd, at : at + 64].astype(BF)
                else:
                    from_rs[h, s, step - 1].wait_recv()
                    out[...] = (
                        gap[zd, h * 128 : h * 128 + 128] + rs_recv[h, s, step - 2].astype(F32)
                    ).astype(BF)
                dst = rs_recv.at[h, s, step - 1]
                if step == 1:
                    out, dst = out.at[half], dst.at[half]
                from_rs[h, s, step] = net.copy(out, dst, net.peer(z=by))

    partial_gap(4)
    rs_step(1)
    partial_gap(3)
    partial_gap(5)
    rs_step(2)
    partial_gap(2)
    partial_gap(6)
    rs_step(3)
    partial_gap(1)
    partial_gap(7)
    rs_step(4)
    partial_gap(0)

    lane = lax.broadcasted_iota(jnp.int32, (1, 256), 1)
    row = lax.div(lane, 128) * 1024 + z * 128 + lax.rem(lane, 128)
    count = jnp.full((1, 256), counts[0], jnp.int32)
    live = (row < count).astype(F32)
    scale = 1.0 / (count.astype(F32) * 1024.0)
    weight = 2.0 * scale * live
    squares = jnp.zeros((64, 256), F32)
    from_ag = {}
    for h in range(2):
        for s, _ in sides:
            from_rs[h, s, 4].wait_recv()
        at = h * 128
        full = (
            gap[z, at : at + 128] + rs_recv[h, 0, 3].astype(F32) + rs_recv[h, 1, 3].astype(F32)
        )
        first, second_half = full[0:64], full[64:128]
        err_a = first * cosine - second_half * sine
        err_b = second_half * cosine + first * sine
        squares = squares + (live * err_a * err_a + live * err_b * err_b) * scale
        err_a, err_b = weight * err_a, weight * err_b
        back[z, at : at + 64] = (err_a * cosine + err_b * sine).astype(BF)
        back[z, at + 64 : at + 128] = (err_b * cosine - err_a * sine).astype(BF)
        slot = back.at[z, at : at + 128]
        for s, by in sides:
            from_ag[h, s, 1] = net.copy(slot, slot, net.peer(z=by))

    def tile_of(value):
        return jnp.broadcast_to(value, (8, 128))

    loss_z[z] = tile_of(jnp.sum(squares, keepdims=True))
    small_z = [net.copy(loss_z.at[z], loss_z.at[z], net.peer(z=d)) for d in RING]

    def add_wgrad(d):
        zo = lax.rem(z + d, 8)
        rows = a_all[pl.ds(zo, 1)].reshape(256, 1024)
        term = jnp.dot(back[zo], rows, preferred_element_type=F32)
        if d == 0:
            w_acc[...] = term
        else:
            w_acc[...] += term

    for step in range(2, 5):
        for h in range(2):
            for s, by in sides:
                from_ag[h, s, step - 1].wait_recv()
                zo = lax.rem(z + (-by * (step - 1)) % 8, 8)
                at = h * 128
                slot = back.at[zo, at : at + 128]
                if step == 4:
                    slot = back.at[zo, at + s * 64 : at + s * 64 + 64]
                from_ag[h, s, step] = net.copy(slot, slot, net.peer(z=by))
        if step == 2:
            add_wgrad(0)
        add_wgrad(step - 1)
        add_wgrad(9 - step)

    for copy in small_z:
        copy.wait_recv()
    loss_g[g] = jnp.sum(loss_z[...], axis=0)
    small_g = [net.copy(loss_g.at[g], loss_g.at[g], net.peer(**o)) for o in GROUP]

    for h in range(2):
        for s, _ in sides:
            from_ag[h, s, 4].wait_recv()
    add_wgrad(4)

    w_send[...] = w_acc[...].reshape(8, 32, 1024).astype(BF)
    from_t = []
    for i, (a, b) in enumerate(TASKS):
        p = net.peer(xh=a, y=b)
        from_t.append(net.copy(w_send.at[p["xh"] * 4 + p["y"]], w_recv.at[i], p))
    for copy in small_g:
        copy.wait_recv()
    loss_t[t] = jnp.sum(loss_g[...], axis=0)
    small_t = [
        net.copy(loss_t.at[t], loss_t.at[t], net.peer(xh=a, y=b)) for a, b in TASKS
    ]
    summed = w_acc[pl.ds(pl.multiple_of(t * 32, 32), 32)]
    for i, copy in enumerate(from_t):
        copy.wait_recv()
        summed = summed + w_recv[i].astype(F32)
    for k in range(4):
        w_piece[k] = summed[:, k * 256 : (k + 1) * 256].astype(BF)
    mine = w_all.at[:, t]
    keep_w = pltpu.make_async_copy(w_piece.at[g], w_all.at[g, t], local_sem.at[3])
    keep_w.start()
    from_w = []
    for offsets in GROUP:
        p = net.peer(**offsets)
        from_w.append(net.copy(w_piece.at[p["xl"] * 2 + p["c"]], w_all.at[g, t], p))
    keep_w.wait()
    for copy in from_w:
        copy.wait_recv()
    from_w2 = [net.copy(mine, mine, net.peer(xh=a, y=b)) for a, b in TASKS]
    for copy in small_t:
        copy.wait_recv()
    loss_out[...] = jnp.sum(loss_t[...], axis=0)
    for copy in from_w2:
        copy.wait_recv()
    for k in range(8):
        block = w_all[k // 2, 4 * (k % 2) : 4 * (k % 2) + 4].reshape(128, 256)
        w_out[:, k * 128 : (k + 1) * 128] = block.astype(F32).T

    net.drain()


def local(hidden, gain, tau, coeff, counts, positions):
    vmem = pl.BlockSpec(memory_space=pltpu.VMEM)
    w, loss = pl.pallas_call(
        kernel,
        out_shape=(
            jax.ShapeDtypeStruct((256, 1024), F32),
            jax.ShapeDtypeStruct((8, 128), F32),
        ),
        in_specs=[pl.BlockSpec(memory_space=pltpu.SMEM)] + [vmem] * 5,
        out_specs=(vmem, vmem),
        scratch_shapes=[
            pltpu.VMEM((8, 64, 1024), BF),
            pltpu.VMEM((8, 2, 2, 64, 1024), BF),
            pltpu.VMEM((4, 256, 256), BF),
            pltpu.VMEM((256, 1024), BF),
            pltpu.VMEM((4, 4, 2, 32, 256), F32),
            pltpu.VMEM((3, 4, 2, 32, 256), F32),
            pltpu.VMEM((4, 2, 32, 256), F32),
            pltpu.VMEM((4, 32, 256), F32),
            pltpu.VMEM((4, 32, 256), BF),
            pltpu.VMEM((4, 2, 32, 1024), BF),
            pltpu.VMEM((8, 256, 256), F32),
            pltpu.VMEM((2, 2, 4, 128, 256), BF),
            pltpu.VMEM((2, 2, 4, 128, 256), BF),
            pltpu.VMEM((8, 256, 256), BF),
            pltpu.VMEM((256, 1024), F32),
            pltpu.VMEM((8, 32, 1024), BF),
            pltpu.VMEM((7, 32, 1024), BF),
            pltpu.VMEM((4, 32, 256), BF),
            pltpu.VMEM((4, 8, 32, 256), BF),
            pltpu.VMEM((2, 2, 8, 128), jnp.int32),
            pltpu.VMEM((8, 8, 128), F32),
            pltpu.VMEM((4, 8, 128), F32),
            pltpu.VMEM((8, 8, 128), F32),
            pltpu.SemaphoreType.DMA((N_SEM,)),
            pltpu.SemaphoreType.DMA((N_SEM,)),
            pltpu.SemaphoreType.DMA((4,)),
        ],
        compiler_params=pltpu.CompilerParams(
            collective_id=0, has_side_effects=True, vmem_limit_bytes=56 * 2**20
        ),
        name="step",
    )(
        counts,
        hidden[0],
        gain.reshape(1, -1),
        tau[0],
        coeff[0],
        jnp.concatenate([positions, positions], axis=1),
    )
    grad = 8192 * 1024 * tau[0].astype(F32) * w
    return grad[None], loss[0, 0]


def solution(mesh):
    spec = P("task", "mp", None)
    return jax.shard_map(
        local,
        mesh=mesh,
        in_specs=(spec, P(), spec, spec, P("task"), P("task", "mp")),
        out_specs=(spec, P()),
        check_vma=False,
    )
```

time: 392 us -> 118 us (0.30); the launches traced: 387 us -> 118 us
  waiting for transfers between devices: 220 us -> 0 us
  blocking collectives: 115 us -> 0 us
  Pallas kernels: 0 us -> 112 us
  between operations: 15.3 us -> 1.29 us
  starting transfers between devices: 11.2 us -> 0 us
  local copies, waits for them, and re-layouts: 9.36 us -> 1.84 us
  matrix products: 6.94 us -> 0 us
  other arithmetic: 9.5 us -> 2.97 us
    psum x6 -> x0, blocking collectives: 115 us -> none  [the longest x1 71.5 us: local(): mixed = lax.psum(coeff[0] * tau_local, TASK)]
    pallas_call x0 -> x1, Pallas kernels: none -> 112 us  [local(): pl.pallas_call(kernel, out_shape=(jax.ShapeDtypeStruct((256, 1024), F32),...]
    reduce_scatter x2 -> x0, waiting for transfers between devices: 103 us -> none  [the longest x1 72.8 us: scatter_pairs(): return lax.psum_scatter(tiles, chips, scatter_dimension=0, tiled=True)[0]]
    all_gather x1 -> x0, waiting for transfers between devices: 73.8 us -> none  [local(): lax.all_gather(back, MP, axis=0, tiled=True)]
    psum x1 -> x0, waiting for transfers between devices: 43.2 us -> none  [local(): wgrad = lax.psum(local_grad, TASK)]
    all_to_all x1 -> x0, starting transfers between devices: 11 us -> none  [local(): lax.all_to_all(normed, MP, split_axis=1, concat_axis=0, tiled=True)]
    dot_general x3 -> x0, matrix products: 6.94 us -> none  [the longest x1 4.43 us: local(): lax.dot_general(block, lax.all_gather(back, MP, axis=0, tiled=True), (((0...]
    another operation x2 -> x0, local copies, waits for them, and re-layouts: 5.4 us -> none  [the longest x1 4.07 us: scatter_pairs(): tiles = tiles.reshape(*sizes, *inside).swapaxes(0, 1).reshape(-1, *inside)]
  transfers between devices with their start and end apart: 5 -> 0, of which waited for: 4 -> 0; matrix products, arithmetic and copies ran while one was open for 0% -> 0% of each run, Pallas kernels for 0% -> 0%
where the time goes in v1:
time: 118 us
  Pallas kernels  112 us (95%)
  other arithmetic  2.97 us (3%)
  local copies, waits for them, and re-layouts  1.84 us (2%)
  between operations  1.29 us (1%)
    pallas_call x1, Pallas kernels, local(): pl.pallas_call(kernel, out_shape=(jax.ShapeDtypeStruct((256, 1024), F32),...  112 us
    broadcast_in_dim x1, other arithmetic, local(): return (grad[None], loss[0, 0])  2.39 us

profile of v1, /device:TPU:1, one launch (start us, length us, event | category | flops | bytes accessed | tf_op | source)
XLA Modules:
  0.0 117.8 jit_solution(6351141986249181268)
XLA Ops:
  1.3 0.0 copy-start.1
  1.3 0.6 copy-done.1
  1.9 0.6 pad_add_fusion.pos
  2.5 0.0 copy-start
  2.5 111.7 %step.1 = (f32[256,1024]{1,0:T(8,128)}, f32[8,128]{1,0:T(8,128)}) custom-call(s32[1]{0:T(128)S(6)} %copy.8.counts, bf16[64,8192]{1,0:T(8,128)(2,1)} %bitcast.9, f32[1,8192]{1,0:T(1,128)} %bitcast.11, bf16[256,1024]{1,0:T(8,128)(2,1)} %bitcast.8, f32[256,1024]{1,0:T(8,128)} %bitcast.10, s32[1,128]{1,0:T(1,128)} %pad_add_fusion.pos), custom_call_target="tpu_custom_call" | custom-call | tf_op jit(solution)/shard_map/step/pallas_call | solution.py:397
  114.2 1.2 %slice.3 = f32[1,1]{1,0:T(1,128)} slice(f32[8,128]{1,0:T(8,128)} %get-tuple-element.5), slice={[0:1], [0:1]} | slice | bytes 8 | tf_op jit(solution)/shard_map/slice | solution.py:446
  115.4 0.0 copy-done
  115.4 2.4 %multiply_bitcast_fusion = f32[1,256,1024]{2,1,0:T(8,128)} fusion(f32[256,1024]{1,0:T(8,128)} %get-tuple-element.4, bf16[1,256,1024]{2,1,0:T(8,128)(2,1)S(1)} %copy-done), kind=kLoop, calls=%fused_computation | loop fusion | flops 786432 | bytes 2621440 | tf_op jit(solution)/shard_map/broadcast_in_dim | solution.py:446
Async XLA Ops:
  1.3 0.7 copy-start.1
  2.5 112.9 %copy-start = (bf16[1,256,1024]{2,1,0:T(8,128)(2,1)S(1)}, bf16[1,256,1024]{2,1,0:T(8,128)(2,1)}, u32[]{:S(2)}) copy-start(bf16[1,256,1024]{2,1,0:T(8,128)(2,1)} %param.8) | copy-start | bytes 1572868

commit v2 on v1

v2 whole, which is shorter than its diff:
```python
import jax
import jax.numpy as jnp
from jax import lax
from jax.experimental import pallas as pl
from jax.experimental.pallas import tpu as pltpu
from jax.sharding import PartitionSpec as P

MESH = pl.DeviceIdType.MESH
BF = jnp.bfloat16
F32 = jnp.float32
HEAD = 128
SIZES = dict(xh=2, y=4, xl=2, z=8, c=2)
GROUP = (dict(c=1), dict(xl=1), dict(xl=1, c=1))
EIGHT = GROUP + tuple(dict(xh=1, **o) for o in (dict(),) + GROUP)
TASKS = tuple(dict(xh=a, y=b) for a in (1, 0) for b in (2, 1, 3, 0) if (a, b) != (0, 0))
RING = (4, 3, 5, 2, 6, 1, 7)
N_SEM = 192


class Links:
    def __init__(self, here, send, recv):
        self.here, self.send, self.recv, self.used, self.open = here, send, recv, 0, []

    def peer(self, **offsets):
        p = dict(self.here)
        for axis, by in offsets.items():
            p[axis] = lax.rem(p[axis] + (by % SIZES[axis]), SIZES[axis])
        return p

    def device(self, p):
        return (p["xh"] * 4 + p["y"], p["xl"] * 16 + p["z"] * 2 + p["c"])

    def copy(self, src, dst, p):
        i = self.used
        self.used += 1
        made = pltpu.make_async_remote_copy(
            src_ref=src,
            dst_ref=dst,
            send_sem=self.send.at[i],
            recv_sem=self.recv.at[i],
            device_id=self.device(p),
            device_id_type=MESH,
        )
        made.start()
        self.open.append(made)
        return made

    def drain(self):
        for made in self.open:
            made.wait_send()


def nt(a, b):
    return lax.dot_general(a, b, (((1,), (1,)), ((), ())), preferred_element_type=F32)


def kernel(
    counts,
    hidden_hbm,
    gain,
    tau_hbm,
    coeff_hbm,
    pos,
    out_hbm,
    loss_out,
    hidden,
    tau,
    coeff,
    ns,
    a_all,
    tau_own,
    tau_t,
    m_own,
    m_recv,
    m_half,
    m_recv2,
    m_piece,
    merged,
    gap,
    rs_send,
    rs_recv,
    back,
    w_acc,
    w_send,
    w_recv,
    w_piece,
    w_all,
    grad,
    pos_all,
    loss_z,
    loss_g,
    loss_t,
    send_sem,
    recv_sem,
    local_sem,
):
    loads = [
        pltpu.make_async_copy(src, dst, local_sem.at[i])
        for i, (src, dst) in enumerate(((tau_hbm, tau), (coeff_hbm, coeff), (hidden_hbm, hidden)))
    ]
    for load in loads:
        load.start()

    t, m = lax.axis_index("task"), lax.axis_index("mp")
    me = dict(
        xh=lax.div(t, 4),
        y=lax.rem(t, 4),
        xl=lax.div(m, 16),
        z=lax.rem(lax.div(m, 2), 8),
        c=lax.rem(m, 2),
    )
    net = Links(me, send_sem, recv_sem)
    xl, z, c, y, xh = me["xl"], me["z"], me["c"], me["y"], me["xh"]
    g = xl * 2 + c

    barrier = pltpu.get_barrier_semaphore()
    partners = [dict(z=d) for d in RING] + list(EIGHT) + [o for o in TASKS if "y" in o and o["y"]]
    for offsets in partners:
        pl.semaphore_signal(
            barrier, inc=1, device_id=net.device(net.peer(**offsets)), device_id_type=MESH
        )

    loads[0].wait()
    loads[1].wait()
    for k in range(8):
        cut = slice(k * 128, (k + 1) * 128)
        tau_f = tau[:, cut].astype(F32)
        mixed_t = (coeff[:, cut] * tau_f).T
        m_own[k // 2, 2 * (k % 2) : 2 * (k % 2) + 2] = mixed_t.reshape(2, 2, 32, 256)
        tau_own[k // 2, (k % 2) * 128 : (k % 2) * 128 + 128] = tau_f.T.astype(BF)

    loads[2].wait()
    total = jnp.zeros((64, 128), F32)
    for k in range(64):
        x = hidden[:, k * 128 : (k + 1) * 128].astype(F32)
        total = total + x * x
    inverse = 1.0 / jnp.sqrt(jnp.sum(total, axis=1, keepdims=True) * (1.0 / 8192.0) + 1e-06)
    inverse = jnp.broadcast_to(inverse, (64, 128))
    for k in range(8):
        for half in range(2):
            for part in range(4):
                at = half * 4096 + k * 512 + part * 128
                x = hidden[:, at : at + 128].astype(F32)
                to = half * 512 + part * 128
                ns[k, :, to : to + 128] = (x * inverse * gain[:, at : at + 128]).astype(BF)

    pl.semaphore_wait(barrier, len(partners))

    from_y = []
    for i, d in enumerate((2, 1, 3)):
        p = net.peer(y=d)
        from_y.append(net.copy(m_own.at[:, p["y"]], m_recv.at[i], p))

    from_z = []
    for d in RING:
        p = net.peer(z=d)
        from_z.append(net.copy(ns.at[p["z"]], a_all.at[z, xl, c], p))
    sib, xn = net.peer(c=1), net.peer(xl=1)
    own_slot = a_all.at[z, xl, c]
    keep = pltpu.make_async_copy(ns.at[z], own_slot, local_sem.at[3])
    keep.start()
    to_sib, to_x, second = [], [], []
    to_sib.append(net.copy(ns.at[z], own_slot, sib))
    to_x.append(net.copy(ns.at[z], own_slot, xn))

    features = pl.ds(pl.multiple_of(g * 256, 256), 256)
    from_tau = []
    for offsets in GROUP:
        p = net.peer(**offsets)
        from_tau.append(net.copy(tau_own.at[p["xl"] * 2 + p["c"]], tau_t.at[:, features], p))
    keep_tau = pltpu.make_async_copy(tau_own.at[g], tau_t.at[:, features], local_sem.at[4])
    keep_tau.start()

    lanes = lax.broadcasted_iota(jnp.int32, (8, 128), 1)
    twice = jnp.concatenate([pos[...], pos[...]], axis=1)
    pos_all[xl, c] = jnp.where(lax.div(lanes, 64) == c, jnp.broadcast_to(twice, (8, 128)), 0)
    small = []
    for offsets in GROUP:
        small.append(net.copy(pos_all.at[xl, c], pos_all.at[xl, c], net.peer(**offsets)))

    def forward(i):
        from_z[i].wait_recv()
        slot = a_all.at[lax.rem(z + (8 - RING[i]), 8), xl, c]
        to_sib.append(net.copy(slot, slot, sib))
        to_x.append(net.copy(slot, slot, xn))

    def pass_on(i):
        to_x[i].wait_recv()
        origin = z if i == 0 else lax.rem(z + (8 - RING[i - 1]), 8)
        slot = a_all.at[origin, 1 - xl, c]
        second.append(net.copy(slot, slot, sib))

    forward(0)
    pass_on(0)

    for copy in small:
        copy.wait_recv()
    halves = (xl, 1 - xl)
    index = lax.broadcasted_iota(jnp.int32, (64, 128), 0).astype(F32)
    freq = jnp.exp(-jnp.log(F32(1000000.0)) * 2.0 * index / HEAD)
    cosine, sine = [], []
    for xr in halves:
        at_rows = pos_all[xr, 0] + pos_all[xr, 1]
        angle = at_rows[0:1].astype(F32) * freq
        cosine.append(jnp.cos(angle))
        sine.append(jnp.sin(angle))

    forward(1)
    forward(2)
    pass_on(1)

    for copy in from_y:
        copy.wait_recv()
    m_half[...] = m_own[:, pl.ds(y, 1)].reshape(4, 2, 32, 256) + m_recv[0] + m_recv[1] + m_recv[2]
    xo = net.peer(xh=1)
    from_xh = net.copy(m_half.at[:, xo["xh"]], m_recv2, xo)

    forward(3)
    pass_on(2)
    pass_on(3)

    from_xh.wait_recv()
    m_piece[...] = (m_half[:, pl.ds(xh, 1)].reshape(4, 32, 256) + m_recv2[...]).astype(BF)
    piece = merged.at[y, xh, :, features]
    keep_m = pltpu.make_async_copy(m_piece.at[g], piece, local_sem.at[5])
    keep_m.start()
    from_eight = []
    for offsets in EIGHT:
        p = net.peer(**offsets)
        from_eight.append(net.copy(m_piece.at[p["xl"] * 2 + p["c"]], piece, p))

    forward(4)
    pass_on(4)

    keep_m.wait()
    for copy in from_eight:
        copy.wait_recv()
    from_y2 = []
    for d in (2, 1, 3):
        from_y2.append(net.copy(merged.at[y], merged.at[y], net.peer(y=d)))

    forward(5)
    pass_on(5)
    forward(6)
    pass_on(6)

    keep.wait()
    keep_tau.wait()
    for copy in from_tau + to_sib + from_y2:
        copy.wait_recv()

    def partial_gap(d, rh):
        zd = lax.rem(z + d, 8)
        rows = a_all[pl.ds(zd, 1), pl.ds(halves[rh], 1)].reshape(128, 1024)
        gap[zd, rh] = nt(merged[...].reshape(256, 1024), rows) - nt(tau_t[...], rows)

    sides = ((0, 1), (1, 7))
    from_rs = {}

    def rs_step(step, rh):
        d = 5 - step
        for h in range(2):
            for s, by in sides:
                zd = lax.rem(z + (by * d) % 8, 8)
                half = slice(s * 64, s * 64 + 64)
                other = slice(64 - s * 64, 128 - s * 64)
                terms = gap[zd, rh, h * 128 : h * 128 + 128]
                out = rs_send.at[rh, h, s, step - 1]
                if step > 1:
                    from_rs[rh, h, s, step - 1].wait_recv()
                came = rs_recv.at[rh, h, s, step - 2]
                if step == 1:
                    out[half] = terms[half].astype(BF)
                elif step == 2:
                    out[half] = (terms[half] + came[half].astype(F32)).astype(BF)
                    out[other] = terms[other].astype(BF)
                else:
                    out[...] = (terms + came[...].astype(F32)).astype(BF)
                dst = rs_recv.at[rh, h, s, step - 1]
                if step == 1:
                    out, dst = out.at[half], dst.at[half]
                from_rs[rh, h, s, step] = net.copy(out, dst, net.peer(z=by))

    partial_gap(4, 0)
    rs_step(1, 0)
    pass_on(7)
    for copy in second:
        copy.wait_recv()
    partial_gap(4, 1)
    rs_step(1, 1)
    for step in (2, 3, 4):
        for rh in range(2):
            partial_gap(5 - step, rh)
            partial_gap(3 + step, rh)
            rs_step(step, rh)
    partial_gap(0, 0)
    partial_gap(0, 1)

    squares = jnp.zeros((64, 128), F32)
    lane = lax.broadcasted_iota(jnp.int32, (1, 128), 1)
    count = jnp.full((1, 128), counts[0], jnp.int32)
    scale = 1.0 / (count.astype(F32) * 1024.0)
    from_ag = {}
    for rh in range(2):
        row = halves[rh] * 1024 + z * 128 + lane
        live = (row < count).astype(F32)
        weight = 2.0 * scale * live
        for h in range(2):
            for s, _ in sides:
                from_rs[rh, h, s, 4].wait_recv()
            at = h * 128
            full = (
                gap[z, rh, at : at + 128]
                + rs_recv[rh, h, 0, 3].astype(F32)
                + rs_recv[rh, h, 1, 3].astype(F32)
            )
            first, last = full[0:64], full[64:128]
            err_a = first * cosine[rh] - last * sine[rh]
            err_b = last * cosine[rh] + first * sine[rh]
            squares = squares + (live * err_a * err_a + live * err_b * err_b) * scale
            err_a, err_b = weight * err_a, weight * err_b
            slot = back.at[z, halves[rh], at : at + 128]
            slot[0:64] = (err_a * cosine[rh] + err_b * sine[rh]).astype(BF)
            slot[64:128] = (err_b * cosine[rh] - err_a * sine[rh]).astype(BF)
            for s, by in sides:
                from_ag[rh, h, s, 1] = net.copy(slot, slot, net.peer(z=by))

    def tile_of(value):
        return jnp.broadcast_to(value, (8, 128))

    loss_z[z] = tile_of(jnp.sum(squares, keepdims=True))
    small_z = [net.copy(loss_z.at[z], loss_z.at[z], net.peer(z=d)) for d in RING]

    def add_wgrad(d):
        zo = lax.rem(z + d, 8)
        rows = a_all[pl.ds(zo, 1)].reshape(256, 1024)
        errors = jnp.concatenate([back[zo, 0], back[zo, 1]], axis=1)
        term = jnp.dot(errors, rows, preferred_element_type=F32)
        if d == 0:
            w_acc[...] = term
        else:
            w_acc[...] += term

    for step in range(2, 5):
        for rh in range(2):
            for h in range(2):
                for s, by in sides:
                    from_ag[rh, h, s, step - 1].wait_recv()
                    zo = lax.rem(z + (-by * (step - 1)) % 8, 8)
                    at, size = h * 128, 128
                    if step == 4:
                        at, size = at + s * 64, 64
                    slot = back.at[zo, halves[rh], at : at + size]
                    from_ag[rh, h, s, step] = net.copy(slot, slot, net.peer(z=by))
        if step == 2:
            add_wgrad(0)
        add_wgrad(step - 1)
        add_wgrad(9 - step)

    for copy in small_z:
        copy.wait_recv()
    loss_g[g] = jnp.sum(loss_z[...], axis=0)
    small_g = [net.copy(loss_g.at[g], loss_g.at[g], net.peer(**o)) for o in GROUP]

    for rh in range(2):
        for h in range(2):
            for s, _ in sides:
                from_ag[rh, h, s, 4].wait_recv()
    add_wgrad(4)

    w_send[...] = w_acc[...].reshape(2, 8, 16, 1024).astype(BF)
    from_t, from_w, from_w2, keep_w = [], [], [], []
    for h in range(2):
        for i, offsets in enumerate(TASKS):
            p = net.peer(**offsets)
            from_t.append(net.copy(w_send.at[h, p["xh"] * 4 + p["y"]], w_recv.at[h, i], p))
    for copy in small_g:
        copy.wait_recv()
    loss_t[t] = jnp.sum(loss_g[...], axis=0)
    small_t = [net.copy(loss_t.at[t], loss_t.at[t], net.peer(**o)) for o in TASKS]
    for h in range(2):
        summed = w_acc[pl.ds(pl.multiple_of(h * 128 + t * 16, 16), 16)]
        for i in range(7):
            from_t[h * 7 + i].wait_recv()
            summed = summed + w_recv[h, i].astype(F32)
        for k in range(4):
            w_piece[h, k] = summed[:, k * 256 : (k + 1) * 256].astype(BF)
        keep_w.append(
            pltpu.make_async_copy(w_piece.at[h, g], w_all.at[g, h, t], local_sem.at[6 + h])
        )
        keep_w[h].start()
        for offsets in GROUP:
            p = net.peer(**offsets)
            from_w.append(
                net.copy(w_piece.at[h, p["xl"] * 2 + p["c"]], w_all.at[g, h, t], p)
            )
    for h in range(2):
        keep_w[h].wait()
        for i in range(3):
            from_w[h * 3 + i].wait_recv()
        mine = w_all.at[:, h, t]
        for offsets in TASKS:
            from_w2.append(net.copy(mine, mine, net.peer(**offsets)))
    for copy in small_t:
        copy.wait_recv()
    loss_out[...] = jnp.sum(loss_t[...], axis=0)[0:1, 0:1]
    stores = []
    for h in range(2):
        for i in range(7):
            from_w2[h * 7 + i].wait_recv()
        for k in range(4):
            cut = slice(k * 256 + h * 128, k * 256 + h * 128 + 128)
            block = w_all[k, h].reshape(128, 256).astype(F32).T
            grad[:, cut] = (8192 * 1024) * tau[:, cut].astype(F32) * block
            store = pltpu.make_async_copy(
                grad.at[:, cut], out_hbm.at[:, cut], local_sem.at[8 + h * 4 + k]
            )
            store.start()
            stores.append(store)
    for store in stores:
        store.wait()
    net.drain()


def local(hidden, gain, tau, coeff, counts, positions):
    vmem = pl.BlockSpec(memory_space=pltpu.VMEM)
    hbm = pl.BlockSpec(memory_space=pl.ANY)
    grad, loss = pl.pallas_call(
        kernel,
        out_shape=(
            jax.ShapeDtypeStruct((256, 1024), F32),
            jax.ShapeDtypeStruct((1, 1), F32),
        ),
        in_specs=[pl.BlockSpec(memory_space=pltpu.SMEM), hbm, vmem, hbm, hbm, vmem],
        out_specs=(hbm, vmem),
        scratch_shapes=[
            pltpu.VMEM((64, 8192), BF),
            pltpu.VMEM((256, 1024), BF),
            pltpu.VMEM((256, 1024), F32),
            pltpu.VMEM((8, 64, 1024), BF),
            pltpu.VMEM((8, 2, 2, 64, 1024), BF),
            pltpu.VMEM((4, 256, 256), BF),
            pltpu.VMEM((256, 1024), BF),
            pltpu.VMEM((4, 4, 2, 32, 256), F32),
            pltpu.VMEM((3, 4, 2, 32, 256), F32),
            pltpu.VMEM((4, 2, 32, 256), F32),
            pltpu.VMEM((4, 32, 256), F32),
            pltpu.VMEM((4, 32, 256), BF),
            pltpu.VMEM((4, 2, 32, 1024), BF),
            pltpu.VMEM((8, 2, 256, 128), F32),
            pltpu.VMEM((2, 2, 2, 4, 128, 128), BF),
            pltpu.VMEM((2, 2, 2, 4, 128, 128), BF),
            pltpu.VMEM((8, 2, 256, 128), BF),
            pltpu.VMEM((256, 1024), F32),
            pltpu.VMEM((2, 8, 16, 1024), BF),
            pltpu.VMEM((2, 7, 16, 1024), BF),
            pltpu.VMEM((2, 4, 16, 256), BF),
            pltpu.VMEM((4, 2, 8, 16, 256), BF),
            pltpu.VMEM((256, 1024), F32),
            pltpu.VMEM((2, 2, 8, 128), jnp.int32),
            pltpu.VMEM((8, 8, 128), F32),
            pltpu.VMEM((4, 8, 128), F32),
            pltpu.VMEM((8, 8, 128), F32),
            pltpu.SemaphoreType.DMA((N_SEM,)),
            pltpu.SemaphoreType.DMA((N_SEM,)),
            pltpu.SemaphoreType.DMA((16,)),
        ],
        compiler_params=pltpu.CompilerParams(
            collective_id=0, has_side_effects=True, vmem_limit_bytes=56 * 2**20
        ),
        name="step",
    )(counts, hidden[0], gain.reshape(1, -1), tau[0], coeff[0], positions)
    return grad[None], loss[0, 0]


def solution(mesh):
    spec = P("task", "mp", None)
    return jax.shard_map(
        local,
        mesh=mesh,
        in_specs=(spec, P(), spec, spec, P("task"), P("task", "mp")),
        out_specs=(spec, P()),
        check_vma=False,
    )
```

time: 118 us -> 110 us (0.932)
  Pallas kernels: 112 us -> 104 us
  other arithmetic: 2.97 us -> 0 us
  between operations: 1.29 us -> 2.97 us
    pallas_call x1, Pallas kernels: 112 us -> 104 us  [local(): pl.pallas_call(kernel, out_shape=(jax.ShapeDtypeStruct((256, 1024), F32),...]
    broadcast_in_dim x1 -> x0, other arithmetic: 2.39 us -> none  [local(): return (grad[None], loss[0, 0])]
    unnamed x4 -> x1, local copies, waits for them, and re-layouts: 0.65 us -> 2.31 us
    slice x1 -> x0, local copies, waits for them, and re-layouts: 1.19 us -> none  [local(): return (grad[None], loss[0, 0])]
where the time goes in v2:
time: 110 us; the launch traced here: 109 us
  Pallas kernels  104 us (95%)
  between operations  2.97 us (3%)
  local copies, waits for them, and re-layouts  2.31 us (2%)
    pallas_call x1, Pallas kernels, local(): pl.pallas_call(kernel, out_shape=(jax.ShapeDtypeStruct((256, 1024), F32),...  104 us
    unnamed x1, local copies, waits for them, and re-layouts  2.31 us

profile of v2, /device:TPU:1, one launch (start us, length us, event | category | flops | bytes accessed | tf_op | source)
XLA Modules:
  0.0 109.4 jit_solution(15313524087704602311)
XLA Ops:
  1.3 104.2 %step.1 = (f32[256,1024]{1,0:T(8,128)}, f32[1,1]{1,0:T(1,128)}) custom-call(s32[1]{0:T(128)S(6)} %copy.10.counts, bf16[64,8192]{1,0:T(8,128)(2,1)} %bitcast.6, f32[1,8192]{1,0:T(1,128)} %bitcast.10, bf16[256,1024]{1,0:T(8,128)(2,1)} %bitcast.9, f32[256,1024]{1,0:T(8,128)} %bitcast.7, s32[1,64]{1,0:T(1,128)} %pos.1), custom_call_target="tpu_custom_call" | custom-call | tf_op jit(solution)/shard_map/step/pallas_call | solution.py:428
  105.4 2.3 %copy.11 = f32[1,256,1024]{2,1,0:T(8,128)} copy(f32[1,256,1024]{2,1,0:T(8,128)} %bitcast.8) | data formatting | bytes 2097152

commit v3 on v2

--- a/solution.py
+++ b/solution.py
@@ -13,8 +13,44 @@
 GROUP = (dict(c=1), dict(xl=1), dict(xl=1, c=1))
 EIGHT = GROUP + tuple(dict(xh=1, **o) for o in (dict(),) + GROUP)
 TASKS = tuple(dict(xh=a, y=b) for a in (1, 0) for b in (2, 1, 3, 0) if (a, b) != (0, 0))
-RING = (4, 3, 5, 2, 6, 1, 7)
+PLANE = tuple(
+    dict(xh=a, y=b, xl=k, c=d)
+    for a in (1, 0)
+    for b in (2, 1, 3, 0)
+    for k in (1, 0)
+    for d in (0, 1)
+    if (a, b, k, d) != (0, 0, 0, 0)
+)
+RING = (1, 7, 2, 6, 3, 5, 4)
 N_SEM = 192
+
+FIRST = 4
+ORDER = (
+    ('q', 0),
+    ('q', 1),
+    ('s', 4),
+    ('s', 5),
+    ('f', 0),
+    ('f', 1),
+    ('t',),
+    ('q', 2),
+    ('q', 3),
+    ('s', 6),
+    ('y',),
+    ('f', 2),
+    ('f', 3),
+    ('e',),
+    ('p', 0),
+    ('p', 1),
+    ('p', 2),
+    ('q', 4),
+    ('q', 5),
+    ('f', 4),
+    ('f', 5),
+    ('q', 6),
+    ('f', 6),
+)
+RSORDER = ("a1", "P", "b1", "a2", "b2", "a3", "b3", "a4", "b4")
 
 
 class Links:
@@ -74,7 +110,6 @@
     m_recv,
     m_half,
     m_recv2,
-    m_piece,
     merged,
     gap,
     rs_send,
@@ -83,7 +118,6 @@
     w_acc,
     w_send,
     w_recv,
-    w_piece,
     w_all,
     grad,
     pos_all,
@@ -114,7 +148,7 @@
     g = xl * 2 + c
 
     barrier = pltpu.get_barrier_semaphore()
-    partners = [dict(z=d) for d in RING] + list(EIGHT) + [o for o in TASKS if "y" in o and o["y"]]
+    partners = [dict(z=d) for d in RING] + list(PLANE)
     for offsets in partners:
         pl.semaphore_signal(
             barrier, inc=1, device_id=net.device(net.peer(**offsets)), device_id_type=MESH
@@ -152,9 +186,13 @@
         from_y.append(net.copy(m_own.at[:, p["y"]], m_recv.at[i], p))
 
     from_z = []
-    for d in RING:
-        p = net.peer(z=d)
+
+    def send_z(i):
+        p = net.peer(z=RING[i])
         from_z.append(net.copy(ns.at[p["z"]], a_all.at[z, xl, c], p))
+
+    for i in range(FIRST):
+        send_z(i)
     sib, xn = net.peer(c=1), net.peer(xl=1)
     own_slot = a_all.at[z, xl, c]
     keep = pltpu.make_async_copy(ns.at[z], own_slot, local_sem.at[3])
@@ -178,11 +216,15 @@
     for offsets in GROUP:
         small.append(net.copy(pos_all.at[xl, c], pos_all.at[xl, c], net.peer(**offsets)))
 
+    def slot_of(i):
+        return a_all.at[lax.rem(z + (8 - RING[i]), 8), xl, c]
+
+    def arrived(i):
+        from_z[i].wait_recv()
+        to_sib.append(net.copy(slot_of(i), slot_of(i), sib))
+
     def forward(i):
-        from_z[i].wait_recv()
-        slot = a_all.at[lax.rem(z + (8 - RING[i]), 8), xl, c]
-        to_sib.append(net.copy(slot, slot, sib))
-        to_x.append(net.copy(slot, slot, xn))
+        to_x.append(net.copy(slot_of(i), slot_of(i), xn))
 
     def pass_on(i):
         to_x[i].wait_recv()
@@ -190,59 +232,42 @@
         slot = a_all.at[origin, 1 - xl, c]
         second.append(net.copy(slot, slot, sib))
 
-    forward(0)
-    pass_on(0)
-
-    for copy in small:
-        copy.wait_recv()
     halves = (xl, 1 - xl)
-    index = lax.broadcasted_iota(jnp.int32, (64, 128), 0).astype(F32)
-    freq = jnp.exp(-jnp.log(F32(1000000.0)) * 2.0 * index / HEAD)
     cosine, sine = [], []
-    for xr in halves:
-        at_rows = pos_all[xr, 0] + pos_all[xr, 1]
-        angle = at_rows[0:1].astype(F32) * freq
-        cosine.append(jnp.cos(angle))
-        sine.append(jnp.sin(angle))
-
-    forward(1)
-    forward(2)
-    pass_on(1)
-
-    for copy in from_y:
-        copy.wait_recv()
-    m_half[...] = m_own[:, pl.ds(y, 1)].reshape(4, 2, 32, 256) + m_recv[0] + m_recv[1] + m_recv[2]
-    xo = net.peer(xh=1)
-    from_xh = net.copy(m_half.at[:, xo["xh"]], m_recv2, xo)
-
-    forward(3)
-    pass_on(2)
-    pass_on(3)
-
-    from_xh.wait_recv()
-    m_piece[...] = (m_half[:, pl.ds(xh, 1)].reshape(4, 32, 256) + m_recv2[...]).astype(BF)
-    piece = merged.at[y, xh, :, features]
-    keep_m = pltpu.make_async_copy(m_piece.at[g], piece, local_sem.at[5])
-    keep_m.start()
-    from_eight = []
-    for offsets in EIGHT:
-        p = net.peer(**offsets)
-        from_eight.append(net.copy(m_piece.at[p["xl"] * 2 + p["c"]], piece, p))
-
-    forward(4)
-    pass_on(4)
-
-    keep_m.wait()
-    for copy in from_eight:
-        copy.wait_recv()
-    from_y2 = []
-    for d in (2, 1, 3):
-        from_y2.append(net.copy(merged.at[y], merged.at[y], net.peer(y=d)))
-
-    forward(5)
-    pass_on(5)
-    forward(6)
-    pass_on(6)
+    from_y2, from_eight = [], []
+
+    def tables():
+        for copy in small:
+            copy.wait_recv()
+        index = lax.broadcasted_iota(jnp.int32, (64, 128), 0).astype(F32)
+        freq = jnp.exp(-jnp.log(F32(1000000.0)) * 2.0 * index / HEAD)
+        for xr in halves:
+            at_rows = pos_all[xr, 0] + pos_all[xr, 1]
+            angle = at_rows[0:1].astype(F32) * freq
+            cosine.append(jnp.cos(angle))
+            sine.append(jnp.sin(angle))
+
+    def sum_y():
+        for copy in from_y:
+            copy.wait_recv()
+        m_half[...] = (
+            m_own[:, pl.ds(y, 1)].reshape(4, 2, 32, 256) + m_recv[0] + m_recv[1] + m_recv[2]
+        )
+        m_recv2[xh, g] = m_half[g]
+        for offsets in EIGHT:
+            p = net.peer(**offsets)
+            from_eight.append(net.copy(m_half.at[p["xl"] * 2 + p["c"]], m_recv2.at[xh, g], p))
+
+    def spread_y():
+        for copy in from_eight:
+            copy.wait_recv()
+        for k in range(4):
+            merged[y, :, :, k * 256 : (k + 1) * 256] = (m_recv2[0, k] + m_recv2[1, k]).astype(BF)
+        for d in (2, 1, 3):
+            from_y2.append(net.copy(merged.at[y], merged.at[y], net.peer(y=d)))
+
+    for what, *i in ORDER:
+        dict(f=forward, q=arrived, p=pass_on, t=tables, y=sum_y, e=spread_y, s=send_z)[what](*i)
 
     keep.wait()
     keep_tau.wait()
@@ -281,18 +306,20 @@
                     out, dst = out.at[half], dst.at[half]
                 from_rs[rh, h, s, step] = net.copy(out, dst, net.peer(z=by))
 
-    partial_gap(4, 0)
-    rs_step(1, 0)
-    pass_on(7)
-    for copy in second:
-        copy.wait_recv()
-    partial_gap(4, 1)
-    rs_step(1, 1)
-    for step in (2, 3, 4):
-        for rh in range(2):
-            partial_gap(5 - step, rh)
+    def step_of(step, rh):
+        partial_gap(5 - step, rh)
+        if step > 1:
             partial_gap(3 + step, rh)
-            rs_step(step, rh)
+        rs_step(step, rh)
+
+    for what in RSORDER:
+        if what == "P":
+            for i in range(len(second), 8):
+                pass_on(i)
+            for copy in second:
+                copy.wait_recv()
+        else:
+            step_of(int(what[1]), "ab".index(what[0]))
     partial_gap(0, 0)
     partial_gap(0, 1)
 
@@ -368,55 +395,41 @@
                 from_ag[rh, h, s, 4].wait_recv()
     add_wgrad(4)
 
-    w_send[...] = w_acc[...].reshape(2, 8, 16, 1024).astype(BF)
-    from_t, from_w, from_w2, keep_w = [], [], [], []
-    for h in range(2):
-        for i, offsets in enumerate(TASKS):
-            p = net.peer(**offsets)
-            from_t.append(net.copy(w_send.at[h, p["xh"] * 4 + p["y"]], w_recv.at[h, i], p))
+    for k in range(4):
+        w_send[k] = w_acc[:, k * 256 : (k + 1) * 256].reshape(8, 32, 256).astype(BF)
+    from_t, from_w2 = [], []
+    for offsets in PLANE:
+        p = net.peer(**offsets)
+        from_t.append(
+            net.copy(
+                w_send.at[p["xl"] * 2 + p["c"], p["xh"] * 4 + p["y"]], w_recv.at[g, t], p
+            )
+        )
+    w_recv[g, t] = w_send[g, t]
     for copy in small_g:
         copy.wait_recv()
     loss_t[t] = jnp.sum(loss_g[...], axis=0)
     small_t = [net.copy(loss_t.at[t], loss_t.at[t], net.peer(**o)) for o in TASKS]
-    for h in range(2):
-        summed = w_acc[pl.ds(pl.multiple_of(h * 128 + t * 16, 16), 16)]
-        for i in range(7):
-            from_t[h * 7 + i].wait_recv()
-            summed = summed + w_recv[h, i].astype(F32)
-        for k in range(4):
-            w_piece[h, k] = summed[:, k * 256 : (k + 1) * 256].astype(BF)
-        keep_w.append(
-            pltpu.make_async_copy(w_piece.at[h, g], w_all.at[g, h, t], local_sem.at[6 + h])
-        )
-        keep_w[h].start()
-        for offsets in GROUP:
-            p = net.peer(**offsets)
-            from_w.append(
-                net.copy(w_piece.at[h, p["xl"] * 2 + p["c"]], w_all.at[g, h, t], p)
-            )
-    for h in range(2):
-        keep_w[h].wait()
-        for i in range(3):
-            from_w[h * 3 + i].wait_recv()
-        mine = w_all.at[:, h, t]
-        for offsets in TASKS:
-            from_w2.append(net.copy(mine, mine, net.peer(**offsets)))
+    for copy in from_t:
+        copy.wait_recv()
+    for k in range(4):
+        w_all[k, t] = jnp.sum(w_recv[k].astype(F32), axis=0).astype(BF)
+    mine = w_all.at[:, t]
+    for offsets in TASKS:
+        from_w2.append(net.copy(mine, mine, net.peer(**offsets)))
     for copy in small_t:
         copy.wait_recv()
     loss_out[...] = jnp.sum(loss_t[...], axis=0)[0:1, 0:1]
+    for copy in from_w2:
+        copy.wait_recv()
     stores = []
-    for h in range(2):
-        for i in range(7):
-            from_w2[h * 7 + i].wait_recv()
-        for k in range(4):
-            cut = slice(k * 256 + h * 128, k * 256 + h * 128 + 128)
-            block = w_all[k, h].reshape(128, 256).astype(F32).T
-            grad[:, cut] = (8192 * 1024) * tau[:, cut].astype(F32) * block
-            store = pltpu.make_async_copy(
-                grad.at[:, cut], out_hbm.at[:, cut], local_sem.at[8 + h * 4 + k]
-            )
-            store.start()
-            stores.append(store)
+    for k in range(8):
+        cut = slice(k * 128, k * 128 + 128)
+        block = w_all[k // 2, 4 * (k % 2) : 4 * (k % 2) + 4].reshape(128, 256).astype(F32).T
+        grad[:, cut] = (8192 * 1024) * tau[:, cut].astype(F32) * block
+        store = pltpu.make_async_copy(grad.at[:, cut], out_hbm.at[:, cut], local_sem.at[8 + k])
+        store.start()
+        stores.append(store)
     for store in stores:
         store.wait()
     net.drain()
@@ -444,18 +457,16 @@
             pltpu.VMEM((4, 4, 2, 32, 256), F32),
             pltpu.VMEM((3, 4, 2, 32, 256), F32),
             pltpu.VMEM((4, 2, 32, 256), F32),
-            pltpu.VMEM((4, 32, 256), F32),
-            pltpu.VMEM((4, 32, 256), BF),
+            pltpu.VMEM((2, 4, 2, 32, 256), F32),
             pltpu.VMEM((4, 2, 32, 1024), BF),
             pltpu.VMEM((8, 2, 256, 128), F32),
             pltpu.VMEM((2, 2, 2, 4, 128, 128), BF),
             pltpu.VMEM((2, 2, 2, 4, 128, 128), BF),
             pltpu.VMEM((8, 2, 256, 128), BF),
             pltpu.VMEM((256, 1024), F32),
-            pltpu.VMEM((2, 8, 16, 1024), BF),
-            pltpu.VMEM((2, 7, 16, 1024), BF),
-            pltpu.VMEM((2, 4, 16, 256), BF),
-            pltpu.VMEM((4, 2, 8, 16, 256), BF),
+            pltpu.VMEM((4, 8, 32, 256), BF),
+            pltpu.VMEM((4, 8, 32, 256), BF),
+            pltpu.VMEM((4, 8, 32, 256), BF),
             pltpu.VMEM((256, 1024), F32),
             pltpu.VMEM((2, 2, 8, 128), jnp.int32),
             pltpu.VMEM((8, 8, 128), F32),

time: 110 us -> 102 us (0.927)
  Pallas kernels: 104 us -> 96.2 us
    pallas_call x1, Pallas kernels: 104 us -> 96.2 us  [local(): pl.pallas_call(kernel, out_shape=(jax.ShapeDtypeStruct((256, 1024), F32),...]
where the time goes in v3:
time: 102 us
  Pallas kernels  96.2 us (94%)
  between operations  2.97 us (3%)
  local copies, waits for them, and re-layouts  2.31 us (2%)
    pallas_call x1, Pallas kernels, local(): pl.pallas_call(kernel, out_shape=(jax.ShapeDtypeStruct((256, 1024), F32),...  96.2 us
    unnamed x1, local copies, waits for them, and re-layouts  2.31 us

profile of v3, /device:TPU:1, one launch (start us, length us, event | category | flops | bytes accessed | tf_op | source)
XLA Modules:
  0.0 101.5 jit_solution(14798140040974882958)
XLA Ops:
  1.3 96.2 %step.1 = (f32[256,1024]{1,0:T(8,128)}, f32[1,1]{1,0:T(1,128)}) custom-call(s32[1]{0:T(128)S(6)} %copy.10.counts, bf16[64,8192]{1,0:T(8,128)(2,1)} %bitcast.6, f32[1,8192]{1,0:T(1,128)} %bitcast.10, bf16[256,1024]{1,0:T(8,128)(2,1)} %bitcast.9, f32[256,1024]{1,0:T(8,128)} %bitcast.7, s32[1,64]{1,0:T(1,128)} %pos.1), custom_call_target="tpu_custom_call" | custom-call | tf_op jit(solution)/shard_map/step/pallas_call | solution.py:441
  97.5 2.3 %copy.11 = f32[1,256,1024]{2,1,0:T(8,128)} copy(f32[1,256,1024]{2,1,0:T(8,128)} %bitcast.8) | data formatting | bytes 2097152

commit v4 on v3

--- a/solution.py
+++ b/solution.py
@@ -44,13 +44,15 @@
     ('p', 1),
     ('p', 2),
     ('q', 4),
+    ('f', 4),
     ('q', 5),
-    ('f', 4),
     ('f', 5),
     ('q', 6),
     ('f', 6),
+    ('p', 3),
+    ('p', 4),
 )
-RSORDER = ("a1", "P", "b1", "a2", "b2", "a3", "b3", "a4", "b4")
+RSORDER = ("a1", "P", "b1", "a2", "b2", "a3", "b3")
 
 
 class Links:
@@ -282,35 +284,46 @@
     sides = ((0, 1), (1, 7))
     from_rs = {}
 
+    def rs_send_to(rh, h, s, slot, by, rows=slice(0, 128)):
+        from_rs[rh, h, s, slot] = net.copy(
+            rs_send.at[rh, h, s, slot, rows], rs_recv.at[rh, h, s, slot, rows], net.peer(z=by)
+        )
+
+    def terms_of(rh, h, d):
+        return gap[lax.rem(z + d % 8, 8), rh, h * 128 : h * 128 + 128]
+
     def rs_step(step, rh):
-        d = 5 - step
+        if step == 1:
+            partial_gap(4, rh)
+            for h in range(2):
+                for s, by in sides:
+                    half = slice(s * 64, s * 64 + 64)
+                    rs_send[rh, h, s, 0, half] = terms_of(rh, h, 4)[half].astype(BF)
+                    rs_send_to(rh, h, s, 0, 2 * by, half)
+            for s, by in sides:
+                partial_gap(3 * by % 8, rh)
+                for h in range(2):
+                    rs_send[rh, h, s, 1] = terms_of(rh, h, 3 * by).astype(BF)
+                    rs_send_to(rh, h, s, 1, by)
+            return
+        d = 4 - step
+        partial_gap(d, rh)
+        partial_gap(8 - d, rh)
         for h in range(2):
             for s, by in sides:
-                zd = lax.rem(z + (by * d) % 8, 8)
-                half = slice(s * 64, s * 64 + 64)
-                other = slice(64 - s * 64, 128 - s * 64)
-                terms = gap[zd, rh, h * 128 : h * 128 + 128]
-                out = rs_send.at[rh, h, s, step - 1]
-                if step > 1:
-                    from_rs[rh, h, s, step - 1].wait_recv()
-                came = rs_recv.at[rh, h, s, step - 2]
-                if step == 1:
-                    out[half] = terms[half].astype(BF)
-                elif step == 2:
-                    out[half] = (terms[half] + came[half].astype(F32)).astype(BF)
-                    out[other] = terms[other].astype(BF)
+                from_rs[rh, h, s, step - 1].wait_recv()
+                terms = terms_of(rh, h, d * by) + rs_recv[rh, h, s, step - 1].astype(F32)
+                if step == 2:
+                    half = slice(s * 64, s * 64 + 64)
+                    other = slice(64 - s * 64, 128 - s * 64)
+                    from_rs[rh, h, s, 0].wait_recv()
+                    rs_send[rh, h, s, 2, half] = (
+                        terms[half] + rs_recv[rh, h, s, 0, half].astype(F32)
+                    ).astype(BF)
+                    rs_send[rh, h, s, 2, other] = terms[other].astype(BF)
                 else:
-                    out[...] = (terms + came[...].astype(F32)).astype(BF)
-                dst = rs_recv.at[rh, h, s, step - 1]
-                if step == 1:
-                    out, dst = out.at[half], dst.at[half]
-                from_rs[rh, h, s, step] = net.copy(out, dst, net.peer(z=by))
-
-    def step_of(step, rh):
-        partial_gap(5 - step, rh)
-        if step > 1:
-            partial_gap(3 + step, rh)
-        rs_step(step, rh)
+                    rs_send[rh, h, s, 3] = terms.astype(BF)
+                rs_send_to(rh, h, s, step, by)
 
     for what in RSORDER:
         if what == "P":
@@ -319,7 +332,7 @@
             for copy in second:
                 copy.wait_recv()
         else:
-            step_of(int(what[1]), "ab".index(what[0]))
+            rs_step(int(what[1]), "ab".index(what[0]))
     partial_gap(0, 0)
     partial_gap(0, 1)
 
@@ -334,7 +347,7 @@
         weight = 2.0 * scale * live
         for h in range(2):
             for s, _ in sides:
-                from_rs[rh, h, s, 4].wait_recv()
+                from_rs[rh, h, s, 3].wait_recv()
             at = h * 128
             full = (
                 gap[z, rh, at : at + 128]

time: 102 us -> 100 us (0.980)
  Pallas kernels: 96.2 us -> 94.8 us
    pallas_call x1, Pallas kernels: 96.2 us -> 94.8 us  [local(): pl.pallas_call(kernel, out_shape=(jax.ShapeDtypeStruct((256, 1024), F32),...]
where the time goes in v4:
time: 100 us
  Pallas kernels  94.8 us (95%)
  between operations  2.97 us (3%)
  local copies, waits for them, and re-layouts  2.31 us (2%)
    pallas_call x1, Pallas kernels, local(): pl.pallas_call(kernel, out_shape=(jax.ShapeDtypeStruct((256, 1024), F32),...  94.8 us
    unnamed x1, local copies, waits for them, and re-layouts  2.31 us

profile of v4, /device:TPU:1, one launch (start us, length us, event | category | flops | bytes accessed | tf_op | source)
XLA Modules:
  0.0 100.1 jit_solution(3991453697561853169)
XLA Ops:
  1.3 94.8 %step.1 = (f32[256,1024]{1,0:T(8,128)}, f32[1,1]{1,0:T(1,128)}) custom-call(s32[1]{0:T(128)S(6)} %copy.10.counts, bf16[64,8192]{1,0:T(8,128)(2,1)} %bitcast.6, f32[1,8192]{1,0:T(1,128)} %bitcast.10, bf16[256,1024]{1,0:T(8,128)(2,1)} %bitcast.9, f32[256,1024]{1,0:T(8,128)} %bitcast.7, s32[1,64]{1,0:T(1,128)} %pos.1), custom_call_target="tpu_custom_call" | custom-call | tf_op jit(solution)/shard_map/step/pallas_call | solution.py:454
  96.1 2.3 %copy.11 = f32[1,256,1024]{2,1,0:T(8,128)} copy(f32[1,256,1024]{2,1,0:T(8,128)} %bitcast.8) | data formatting | bytes 2097152

commit v5 on v4

--- a/solution.py
+++ b/solution.py
@@ -381,6 +381,7 @@
         else:
             w_acc[...] += term
 
+    add_wgrad(0)
     for step in range(2, 5):
         for rh in range(2):
             for h in range(2):
@@ -392,8 +393,6 @@
                         at, size = at + s * 64, 64
                     slot = back.at[zo, halves[rh], at : at + size]
                     from_ag[rh, h, s, step] = net.copy(slot, slot, net.peer(z=by))
-        if step == 2:
-            add_wgrad(0)
         add_wgrad(step - 1)
         add_wgrad(9 - step)
 

time: 100 us -> 100 us (level)
  no operation moved by 1% of the time
where the time goes in v5:
time: 100 us
  Pallas kernels  94.9 us (95%)
  between operations  2.97 us (3%)
  local copies, waits for them, and re-layouts  2.31 us (2%)
    pallas_call x1, Pallas kernels, local(): pl.pallas_call(kernel, out_shape=(jax.ShapeDtypeStruct((256, 1024), F32),...  94.9 us
    unnamed x1, local copies, waits for them, and re-layouts  2.31 us

profile of v5, /device:TPU:1, one launch (start us, length us, event | category | flops | bytes accessed | tf_op | source)
XLA Modules:
  0.0 100.2 jit_solution(417440903302341299)
XLA Ops:
  1.3 94.9 %step.1 = (f32[256,1024]{1,0:T(8,128)}, f32[1,1]{1,0:T(1,128)}) custom-call(s32[1]{0:T(128)S(6)} %copy.10.counts, bf16[64,8192]{1,0:T(8,128)(2,1)} %bitcast.6, f32[1,8192]{1,0:T(1,128)} %bitcast.10, bf16[256,1024]{1,0:T(8,128)(2,1)} %bitcast.9, f32[256,1024]{1,0:T(8,128)} %bitcast.7, s32[1,64]{1,0:T(1,128)} %pos.1), custom_call_target="tpu_custom_call" | custom-call | tf_op jit(solution)/shard_map/step/pallas_call | solution.py:453
  96.2 2.3 %copy.11 = f32[1,256,1024]{2,1,0:T(8,128)} copy(f32[1,256,1024]{2,1,0:T(8,128)} %bitcast.8) | data formatting | bytes 2097152
